TPU v7x, 256 devices: a whole 4x4x8 slice. The times are simulated.
256 devices in a mesh: ctx: 32 (over y, z_lo, core), ch: 8 (over z_hi, x).
Axes of the slice: x: 4, y: 4, z: 8 (z_hi: 2, z_lo: 4; z = z_hi * 4 + z_lo), core: 2. Of those that a mesh axis runs over, the one named last changes fastest.
Arguments:
- token_ids: int32 [16384], P('ctx'), may hold values from 65 to 84, as said below
- embedding: bfloat16 [512, 4096], P(None, 'ch'), may hold values from -6 to 6
- long_table: bfloat16 [512, 3, 4096], P(None, None, 'ch'), may hold values from -6 to 6
- long_taps: float32 [3, 3, 4096], P(None, None, 'ch'), may hold values from -3 to 3
- long_residue: float32 [256, 16], P('ch'), may hold values from -1.5 to 1.5
- long_rate: float32 [256, 16], P('ch'), may hold values from 1.2207031e-06 to 0.04
- long_skip: float32 [4096], P('ch'), may hold values from 0.25 to 1.75
- medium_gain: bfloat16 [4096], P('ch'), may hold values from 0.25 to 1.75
- medium_weight: bfloat16 [4096, 3, 4096], P('ctx', None, 'ch'), may hold values from -0.09375 to 0.09375
- medium_taps: float32 [3, 3, 4096], P(None, None, 'ch'), may hold values from -3 to 3
- medium_group_filter: float32 [256, 128], P('ch'), may hold values from -0.6 to 0.6
- medium_skip: float32 [4096], P('ch'), may hold values from 0.25 to 1.75
- filter_group: int32 [4096], P('ch'), may hold values from 0 to 255, as said below
Outputs:
- block_output: bfloat16 [16384, 4096], P('ctx', 'ch')
Inputs may be any that keep to these rules, and one draw needn't show every extreme that they name: `token_ids`: every token is the byte code of A, C, G, T or N. `filter_group`: each filter group has exactly 16 channels, all within one block of 512 consecutive channels; block j holds groups j * (32) to (j + 1) * 32 - 1.
All inputs are finite; a program needn't handle non-finite values.
Results may differ from a plain program's by a relative error of at most 0.006.
Values may be sent and summed in bfloat16 or wider, within the bound.
A program may use at most 128 MiB of HBM per device.

v0:
```python
import jax
import jax.numpy as jnp
from jax import lax
from jax.sharding import PartitionSpec as P

MODEL_WIDTH = 4096


epsilon = 1e-06


def from_behind(x, axis, by):
    count = lax.axis_size(axis)
    pairs = [(i, i + by) for i in range(count) if 0 <= i + by < count]
    return lax.ppermute(x, axis, pairs)


def carried_in(value, axis, join, neutral):
    count, mine = (lax.axis_size(axis), lax.axis_index(axis))
    pieces = jax.tree.map(lambda part: lax.all_gather(part, axis), value)
    running = jax.tree.map(
        lambda part, zero: jnp.full_like(part, 0) + jnp.asarray(zero, part.dtype), value, neutral
    )

    def turn(position, running):
        longer = join(running, jax.tree.map(lambda part: part[position], pieces))
        return jax.tree.map(lambda new, old: jnp.where(position < mine, new, old), longer, running)

    return lax.fori_loop(0, count - 1, turn, running)


def featurize(streams, before, filter_taps):
    extended = jnp.concatenate([before, streams], axis=0).astype(jnp.float32)
    length = streams.shape[0]
    mixed = filter_taps[0] * extended[2 : 2 + length]
    mixed = mixed + filter_taps[1] * extended[1 : 1 + length]
    mixed = mixed + filter_taps[2] * extended[0:length]
    return mixed


def previous_rows(values, count):
    return from_behind(values[values.shape[0] - count :], "ctx", 1)


def chain_combine(earlier, later):
    return (earlier[0] * later[0], earlier[1] * later[0] + later[1])


def split_product(form, data, table):
    upper = table.astype(jnp.bfloat16)
    lower = (table - upper.astype(jnp.float32)).astype(jnp.bfloat16)
    first = jnp.einsum(form, data, upper, preferred_element_type=jnp.float32)
    return first + jnp.einsum(form, data, lower, preferred_element_type=jnp.float32)


def local(
    token_ids,
    embedding,
    long_table,
    long_taps,
    long_residue,
    long_rate,
    long_skip,
    medium_gain,
    medium_weight,
    medium_taps,
    medium_group_filter,
    medium_skip,
    filter_group,
):
    tokens = token_ids.shape[0]
    channels = embedding.shape[1]
    vocab = embedding.shape[0]
    groups = long_rate.shape[0]
    pole_count = long_rate.shape[1]
    tap_count = medium_group_filter.shape[1]
    members = channels // groups
    blocks = tokens // tap_count
    one_hot = (token_ids[:, None] == jnp.arange(vocab, dtype=jnp.int32)[None, :]).astype(
        jnp.bfloat16
    )
    resid = jnp.dot(one_hot, embedding, preferred_element_type=jnp.float32)
    streams = jnp.dot(
        one_hot, long_table.reshape(vocab, 3 * channels), preferred_element_type=jnp.float32
    )
    streams = streams.astype(jnp.bfloat16).reshape(tokens, 3, channels)
    local_group = filter_group - lax.axis_index("ch") * groups
    channel_ids = jnp.arange(channels, dtype=jnp.int32)
    same_group = local_group[:, None] == local_group[None, :]
    rank_within = jnp.sum(same_group & (channel_ids[None, :] < channel_ids[:, None]), axis=1)
    placed = local_group * members + rank_within
    select = placed[:, None] == channel_ids[None, :]
    select_half = select.astype(jnp.bfloat16)
    select_wide = select.astype(jnp.float32)

    def grouped(values):
        length = values.shape[0]
        moved = jnp.dot(values, select_half, preferred_element_type=jnp.float32).astype(
            jnp.bfloat16
        )
        return moved.reshape(length, groups, members).transpose(1, 2, 0)

    def ungrouped(values):
        length = values.shape[-1]
        flat = values.transpose(2, 0, 1).reshape(length, channels)
        return jnp.dot(
            flat, select_wide.T, precision=lax.Precision.HIGHEST, preferred_element_type=jnp.float32
        )

    before = previous_rows(streams, 2)
    mixed = featurize(streams, before, long_taps)
    query = mixed[:, 0]
    product = (mixed[:, 1] * mixed[:, 2]).astype(jnp.bfloat16)
    product_wide = product.astype(jnp.float32)
    positions = jnp.arange(tap_count, dtype=jnp.float32)
    weight_res = long_residue * jnp.sqrt(-jnp.expm1(-2.0 * long_rate))
    kernel = jnp.sum(weight_res[:, :, None] * jnp.exp(-long_rate[:, :, None] * positions), axis=1)
    offsets = jnp.arange(tap_count, dtype=jnp.int32)
    lag = offsets[None, :] - offsets[:, None]
    toeplitz = jnp.where(lag[None] >= 0, kernel[:, jnp.clip(lag, 0, tap_count - 1)], 0.0)
    blocked = grouped(product).reshape(groups, members, blocks, tap_count)
    inner = split_product("gcns,gst->gcnt", blocked, toeplitz)
    ending = jnp.exp(-long_rate[:, :, None] * (tap_count - 1.0 - positions))
    closing = split_product("gcns,gps->gcnp", blocked, ending)
    across = jnp.exp(-long_rate * tap_count)[:, None, :]
    summary = jnp.zeros((groups, members, pole_count), jnp.float32)
    for block in range(blocks):
        summary = summary * across + closing[:, :, block]
    whole_decay = jnp.broadcast_to(
        jnp.exp(-long_rate * tokens)[:, None, :], (groups, members, pole_count)
    )
    decay_flat = whole_decay.transpose(2, 0, 1).reshape(pole_count, channels)
    summary_flat = summary.transpose(2, 0, 1).reshape(pole_count, channels)
    identity = (
        jnp.ones((pole_count, channels), jnp.float32),
        jnp.zeros((pole_count, channels), jnp.float32),
    )
    carried = carried_in((decay_flat, summary_flat), "ctx", chain_combine, identity)[1]
    state = carried.reshape(pole_count, groups, members).transpose(1, 2, 0)
    starts = []
    for block in range(blocks):
        starts.append(state)
        state = state * across + closing[:, :, block]
    start_stack = jnp.stack(starts, axis=2)
    entry = weight_res[:, :, None] * jnp.exp(-long_rate[:, :, None] * (positions + 1.0))
    outer = jnp.einsum("gcnp,gpt->gcnt", start_stack, entry, precision=lax.Precision.HIGHEST)
    conv_long = (
        ungrouped((inner + outer).reshape(groups, members, tokens)) + long_skip * product_wide
    )
    middle = (resid + query * conv_long).astype(jnp.bfloat16)
    middle_wide = middle.astype(jnp.float32)
    squares = lax.psum(jnp.sum(middle_wide * middle_wide, axis=1), "ch")
    scale = lax.rsqrt(squares / MODEL_WIDTH + epsilon)
    normed = (middle_wide * scale[:, None] * medium_gain.astype(jnp.float32)).astype(jnp.bfloat16)
    features = lax.all_gather(normed, "ch", axis=1, tiled=True)
    piece = lax.all_gather(medium_weight, "ctx", axis=0, tiled=True)
    projected = jnp.dot(
        features, piece.reshape(piece.shape[0], 3 * channels), preferred_element_type=jnp.float32
    )
    projected = projected.astype(jnp.bfloat16).reshape(tokens, 3, channels)
    before2 = previous_rows(projected, 2)
    mixed2 = featurize(projected, before2, medium_taps)
    product2 = (mixed2[:, 1] * mixed2[:, 2]).astype(jnp.bfloat16)
    margin = previous_rows(product2, tap_count)
    query2 = mixed2[:, 0]
    second_product_wide = product2.astype(jnp.float32)
    extended = jnp.concatenate([margin, product2], axis=0)
    framed = grouped(extended).reshape(groups, members, blocks + 1, tap_count)
    windows = jnp.concatenate([framed[:, :, :-1], framed[:, :, 1:]], axis=-1)
    wide_offsets = jnp.arange(2 * tap_count, dtype=jnp.int32)
    tap_delay = offsets[None, :] + tap_count - wide_offsets[:, None]
    valid = (tap_delay >= 0) & (tap_delay < tap_count)
    banded = jnp.where(
        valid[None], medium_group_filter[:, jnp.clip(tap_delay, 0, tap_count - 1)], 0.0
    )
    medium = split_product("gcns,gst->gcnt", windows, banded)
    medium_convolution = (
        ungrouped(medium.reshape(groups, members, tokens)) + medium_skip * second_product_wide
    )
    return (middle_wide + query2 * medium_convolution).astype(jnp.bfloat16)


def solution(mesh):
    in_specs = (
        P("ctx"),
        P(None, "ch"),
        P(None, None, "ch"),
        P(None, None, "ch"),
        P("ch", None),
        P("ch", None),
        P("ch"),
        P("ch"),
        P("ctx", None, "ch"),
        P(None, None, "ch"),
        P("ch", None),
        P("ch"),
        P("ch"),
    )
    out_specs = P("ctx", "ch")
    return jax.shard_map(local, mesh=mesh, in_specs=in_specs, out_specs=out_specs, check_vma=False)
```

profile of v0, /device:TPU:49, one launch (start us, length us, event | category | flops | bytes accessed | tf_op | source)
XLA Modules:
  0.0 560.7 jit_solution(1877062003630645721)
XLA Ops:
  6.5 1.8 copy.92
  10.9 4.1 collective-permute-start
  16.3 1.7 copy.94
  18.3 1.4 collective-permute-done
  20.6 2.8 fusion.4
  27.4 54.5 %gather_fusion = f32[16384,32]{1,0:T(8,128)} fusion(f32[32,128]{0,1:T(8,128)S(1)} %copy.97, s32[16384]{0:T(1024)S(1)} %fusion.91), kind=kCustom, calls=%fused_computation | custom fusion | bytes 4259840 | tf_op jit(solution)/shard_map/gather | solution.py:120
  81.9 5.5 copy.98
  87.5 1.6 fusion.44
  90.5 44.1 %all-gather.7.cloned.1.call-done = f32[32,16,512]{2,1,0:T(8,128)} async-done(((f32[1,16,512]{2,1,0:T(8,128)}), f32[32,16,512]{2,1,0:T(8,128)}) %all-gather.7.cloned.1.call-update) | async-done | bytes 1048592 | tf_op jit(solution)/shard_map/all_gather | solution.py:20
  134.7 25.2 %while.14 = (s32[]{:T(128)}, f32[16,512]{1,0:T(8,128)S(1)}, s32[]{:T(128)}, f32[32,16,512]{2,1,0:T(8,128)}, f32[32,16,512]{2,1,0:T(8,128)}, /*index=5*/s32[]{:T(128)}, s32[]{:T(128)}) while((s32[]{:T(128)}, f32[16,512]{1,0:T(8,128)S(1)}, s32[]{:T(128)}, f32[32,16,512]{2,1,0:T(8,128)}, f32[32,16,512]{2,1,0:T(8,128)}, ...), condition=%wide.region_3.4_spmd.clone, body=%wide.region_2.3_spmd.clone.sunk | while | flops 32772 | bytes 131173 | solution.py:29
  163.8 2.6 fusion.28
  166.3 26.1 %psum.7 = f32[512]{0:T(512)S(1)} all-reduce(f32[512]{0:T(512)S(1)} %get-tuple-element.144), channel_id=1, replica_groups=mesh['ctx'=32,'ch'=8] {'ch'}, use_global_device_ids=true, to_apply=%region_5.6 | all-reduce | flops 512 | bytes 4096 | tf_op jit(solution)/shard_map/psum | solution.py:152
  194.7 103.3 %all-gather.9.cloned.1.call-done = bf16[512,4096]{0,1:T(8,128)(2,1)} async-done(((bf16[512,512]{0,1:T(8,128)(2,1)}), bf16[512,4096]{0,1:T(8,128)(2,1)}) %all-gather.9.cloned.1.call-update) | async-done | bytes 4194320 | tf_op jit(solution)/shard_map/all_gather | solution.py:155
  298.0 101.5 %all-gather.11.cloned.1.call-done = bf16[4096,3,512]{0,2,1:T(8,128)(2,1)} async-done(((bf16[128,3,512]{0,2,1:T(8,128)(2,1)}), bf16[4096,3,512]{0,2,1:T(8,128)(2,1)}) %all-gather.11.cloned.1.call-update) | async-done | bytes 12582928 | tf_op jit(solution)/shard_map/all_gather | solution.py:156
  399.5 11.0 %convolution_convert_fusion = bf16[512,1536]{1,0:T(8,128)(2,1)S(1)} fusion(bf16[512,4096]{0,1:T(8,128)(2,1)} %all-gather.9.cloned.1.call-done, bf16[4096,1536]{0,1:T(8,128)(2,1)} %bitcast.244), kind=kOutput, calls=%fused_computation.18 | convolution fusion | flops 6443237376 | bytes 18350080 | tf_op jit(solution)/shard_map/dot_general | solution.py:157
  411.9 3.7 collective-permute-start.1
  415.8 108.5 %gather_fusion.1 = f32[32768,32]{1,0:T(8,128)} fusion(f32[32,128]{0,1:T(8,128)S(1)} %copy.117, s32[32768]{0:T(1024)S(1)} %fusion.78), kind=kCustom, calls=%fused_computation.1 | custom fusion | bytes 8519680 | tf_op jit(solution)/shard_map/gather | solution.py:174
  524.2 11.8 %copy.118 = f32[256,128,32]{1,0,2:T(8,128)} copy(f32[256,128,32]{2,1,0:T(8,128)} %bitcast.227) | data formatting | bytes 8388608 | tf_op jit(solution)/shard_map/gather | solution.py:174
  536.0 1.7 copy.114
  538.6 2.8 fusion.2
  541.6 2.4 collective-permute-start.2
  544.1 1.5 collective-permute-done.2
  547.8 1.5 copy-done.2
  550.7 2.4 fusion.31
  (144 shorter events, 48.0 us)
Async XLA Ops:
  6.5 81.0 %copy-start = (bf16[512,512]{1,0:T(8,128)(2,1)S(1)}, bf16[512,512]{1,0:T(8,128)(2,1)}, u32[]{:S(2)}) copy-start(bf16[512,512]{1,0:T(8,128)(2,1)} %param.16) | copy-start | bytes 1572868
  6.5 1.8 copy-start.19
  6.5 84.0 %all-gather.5.cloned.1.call-start = ((), (), s32[]{:S(2)}) async-start(), calls=%async_computation | async-start | bytes 1081344 | tf_op jit(solution)/shard_map/all_gather | solution.py:20
  8.3 6.7 %copy-start.16 = (f32[32,16]{0,1:T(8,128)S(1)}, f32[32,16]{0,1:T(8,128)}, u32[]{:S(2)}) copy-start(f32[32,16]{0,1:T(8,128)} %param.19) | copy-start | bytes 6148
  8.3 6.7 %copy-start.17 = (f32[32,16]{0,1:T(8,128)S(1)}, f32[32,16]{0,1:T(8,128)}, u32[]{:S(2)}) copy-start(f32[32,16]{0,1:T(8,128)} %param.20) | copy-start | bytes 6148
  8.4 7.7 %copy-start.13 = (f32[3,3,512]{2,1,0:T(4,128)S(1)}, f32[3,3,512]{2,1,0:T(4,128)}, u32[]{:S(2)}) copy-start(f32[3,3,512]{2,1,0:T(4,128)} %param.18) | copy-start | bytes 55300
  8.4 7.7 %copy-start.18 = (s32[512]{0:T(512)S(1)}, s32[512]{0:T(512)}, u32[]{:S(2)}) copy-start(s32[512]{0:T(512)} %param.27) | copy-start | bytes 6148
  10.9 8.8 %collective-permute-start = (bf16[2,3,512]{0,2,1:T(8,128)(2,1)S(1)}, bf16[2,3,512]{0,2,1:T(8,128)(2,1)S(1)}, u32[]{:S(2)}, u32[]{:S(2)}) collective-permute-start(bf16[2,3,512]{0,2,1:T(8,128)(2,1)S(1)} %bitcast.242), channel_id=1, source_target_pairs={{0,8},{8,16},{16,24},{24,32},{32,40},{40,48},{48,56},{56,64},{64,7... | collective-permute-start | bytes 18440 | tf_op jit(solution)/shard_map/ppermute | solution.py:15
  16.0 118.7 %all-gather.7.cloned.1.call-start = ((), (), s32[]{:S(2)}) async-start(), calls=%async_computation.1 | async-start | bytes 1081344 | tf_op jit(solution)/shard_map/all_gather | solution.py:20
  23.3 1.9 copy-start.4
  26.9 271.1 %all-gather.9.cloned.1.call-start = ((), (), s32[]{:S(2)}) async-start(), calls=%async_computation.2 | async-start | bytes 4718592 | tf_op jit(solution)/shard_map/all_gather | solution.py:155
  81.9 5.5 copy-start.22
  159.9 2.4 copy-start.7
  162.4 1.3 copy-start.9
  162.4 1.3 copy-start.20
  163.0 30.6 %copy-start.12 = (bf16[128,3,512]{2,0,1:T(8,128)(2,1)S(1)}, bf16[128,3,512]{2,0,1:T(8,128)(2,1)}, u32[]{:S(2)}) copy-start(bf16[128,3,512]{2,0,1:T(8,128)(2,1)} %param.23) | copy-start | bytes 1179652
  193.4 206.1 %all-gather.11.cloned.1.call-start = ((), (), s32[]{:S(2)}) async-start(), calls=%async_computation.3 | async-start | bytes 12976128 | tf_op jit(solution)/shard_map/all_gather | solution.py:156
  399.5 16.1 %copy-start.14 = (f32[3,3,512]{2,1,0:T(4,128)S(1)}, f32[3,3,512]{2,1,0:T(4,128)}, u32[]{:S(2)}) copy-start(f32[3,3,512]{2,1,0:T(4,128)} %param.24) | copy-start | bytes 55300
  399.5 16.1 %copy-start.15 = (f32[32,128]{1,0:T(8,128)S(1)}, f32[32,128]{1,0:T(8,128)}, u32[]{:S(2)}) copy-start(f32[32,128]{1,0:T(8,128)} %param.25) | copy-start | bytes 49156
  411.9 125.8 %collective-permute-start.1 = (bf16[2,3,512]{0,2,1:T(8,128)(2,1)S(1)}, bf16[2,3,512]{0,2,1:T(8,128)(2,1)S(1)}, u32[]{:S(2)}, u32[]{:S(2)}) collective-permute-start(bf16[2,3,512]{0,2,1:T(8,128)(2,1)S(1)} %bitcast.243), channel_id=1, source_target_pairs={{0,8},{8,16},{16,24},{24,32},{32,40},{40,48},{48,56},{56,64},{64,7... | collective-permute-start | bytes 18440 | tf_op jit(solution)/shard_map/ppermute | solution.py:15
  541.4 5.0 copy-start.3
  541.6 4.1 collective-permute-start.2
  547.1 2.2 copy-start.2
  549.8 4.4 copy-start.1
  (6 other events, 6.5 us)
Sparse Core Ops, SparseCore 0:
  16.1 59.0 all-gather.4
  77.0 57.6 all-gather.6
  193.5 104.4 all-gather.8
  299.6 99.8 all-gather.10
where the time goes:
time: 568 us; the launch traced here: 561 us
  waiting for transfers between devices  252 us (44%)
  local copies, waits for them, and re-layouts  198 us (35%)
  other arithmetic  35.1 us (6%)
  blocking collectives  26.1 us (5%)
  matrix products  24.8 us (4%)
  between operations  13.8 us (2%)
  starting transfers between devices  10.5 us (2%)
    gather x2, local copies, waits for them, and re-layouts, local(): medium_group_filter[:, jnp.clip(tap_delay, 0, tap_count - 1)]  120 us
    all_gather x1, waiting for transfers between devices, local(): features = lax.all_gather(normed, 'ch', axis=1, tiled=True)  103 us
    all_gather x1, waiting for transfers between devices, local(): piece = lax.all_gather(medium_weight, 'ctx', axis=0, tiled=True)  101 us
    gather x2, local copies, waits for them, and re-layouts, local(): kernel[:, jnp.clip(lag, 0, tap_count - 1)]  60 us
    all_gather x2, waiting for transfers between devices, carried_in(): pieces = jax.tree.map(lambda part: lax.all_gather(part, axis), value)  44.1 us
    psum x1, blocking collectives, local(): squares = lax.psum(jnp.sum(middle_wide * middle_wide, axis=1), 'ch')  26.1 us
    select_n x31, other arithmetic, turn(): jnp.where(position < mine, new, old)  24.4 us
  transfers between devices with their start and end apart: 7, of which 5 were waited for; matrix products, arithmetic and copies ran while one was open for 35% of the time, Pallas kernels for 0%

commit v1 on v0

v1 whole, which is shorter than its diff:
```python
import functools

import jax
import jax.numpy as jnp
from jax import lax
from jax.experimental import pallas as pl
from jax.experimental.pallas import tpu as pltpu
from jax.sharding import PartitionSpec as P

EPSILON = 1e-06
HALO = 144
F32 = jnp.float32
BF16 = jnp.bfloat16


def kernel(
    sizes,
    token_ref,
    emb_ref,
    table_ref,
    ltaps_ref,
    residue_ref,
    rate_ref,
    lskip_ref,
    gain_ref,
    w_ref,
    mtaps_ref,
    filt_ref,
    mskip_ref,
    group_ref,
    out_ref,
    emb,
    table,
    tok_ref,
    weights,
    feats,
    acc,
    hot,
    halo_tok,
    prod,
    query,
    resid,
    conv,
    chan,
    excl,
    end_own,
    end_other,
    chip_own,
    chip_all,
    row_own,
    row_all,
    note_own,
    note_all,
    scale,
    half_norm,
    perm,
    toep,
    tail_out,
    tail_in,
    prod2,
    turned,
    conv_hi,
    conv_lo,
    load_sem,
    tok_sem,
    z_sem,
    y_sem,
    pair_sem,
    end_sem,
    chip_sem,
    row_sem,
    note_sem,
    x_sem,
    far_sem,
    tail_sem,
):
    ny, nz, nh, nx = sizes
    nch = nh * nx
    tokens, width = query.shape
    piece = w_ref.shape[1]
    ctx, ch = lax.axis_index("ctx"), lax.axis_index("ch")
    core, chip = ctx % 2, ctx // 2
    z, y = chip % nz, chip // nz
    x, h = ch % nx, ch // nx
    last_ctx = 2 * ny * nz - 1
    waits = []

    def along(yy, zz, cc):
        return {"ctx": (yy * nz + zz) * 2 + cc}

    def across(hh, xx):
        return {"ch": hh * nx + xx}

    def copy(src, dst, sems, to):
        made = pltpu.make_async_remote_copy(
            src_ref=src,
            dst_ref=dst,
            send_sem=sems[0],
            recv_sem=sems[1],
            device_id=to,
            device_id_type=pl.DeviceIdType.MESH,
        )
        return made

    def send(make, cond=None):
        copy(*make()).start()
        waits.append((make, cond))

    def sems_of(ref, *index):
        return ref.at[(0, *index)], ref.at[(1, *index)]

    def arrived(dst, sems, to):
        copy(dst, dst, sems, to).wait_recv()

    barrier = pltpu.get_barrier_semaphore()
    peers = [along(y, z, 1 - core)]
    peers += [along(y, (z + o) % nz, core) for o in range(1, nz)]
    peers += [along((y + o) % ny, z, core) for o in range(1, ny)]
    peers += [{"ch": (ch + o) % nch} for o in range(1, nch)]
    for peer in peers:
        pl.semaphore_signal(barrier, inc=1, device_id=peer, device_id_type=pl.DeviceIdType.MESH)
    has_next = jnp.logical_and(core == 1, ctx < last_ctx)
    has_before = jnp.logical_and(core == 0, ctx > 0)

    @pl.when(has_next)
    def _():
        pl.semaphore_signal(
            barrier, inc=1, device_id={"ctx": ctx + 1}, device_id_type=pl.DeviceIdType.MESH
        )

    @pl.when(has_before)
    def _():
        pl.semaphore_signal(
            barrier, inc=1, device_id={"ctx": ctx - 1}, device_id_type=pl.DeviceIdType.MESH
        )

    def rows_of(slot):
        return pl.ds(pl.multiple_of(slot * piece, piece), piece)

    def part_of(slot, part):
        return pl.ds(pl.multiple_of(slot * piece + part * (piece // 2), piece // 2), piece // 2)

    loads = [
        pltpu.make_async_copy(
            w_ref.at[i], weights.at[rows_of(ctx), pl.ds(i * width, width)], load_sem.at[i]
        )
        for i in range(3)
    ]
    loads.append(pltpu.make_async_copy(emb_ref.at[pl.ds(64, 32)], emb, load_sem.at[3]))
    loads.append(pltpu.make_async_copy(table_ref.at[:, pl.ds(64, 32)], table, load_sem.at[4]))
    for load in loads:
        load.start()
    tok_ref[...] = jnp.broadcast_to(token_ref[...], tok_ref.shape)

    def slot(yy, zz, cc):
        return (yy * nz + zz) * 2 + cc

    def event_of(e):
        if e == 0:
            return z, None
        r = (e - 1) // 2
        if e % 2 == 1:
            return z - 1 - r, lambda: z - 1 - r >= 0
        return z + 1 + r, lambda: z + 1 + r < nz

    def guarded(cond, body):
        if cond is None:
            body()
        else:
            pl.when(cond())(body)

    up, down = (y + 1) % ny, (y + ny - 1) % ny

    def pair(e, kind, rows, cond):
        def make():
            view = weights.at[rows()]
            return view, view, sems_of(pair_sem, e, kind), along(y, z, 1 - core)

        send(make, cond)

    def y_sends(e, zz, cond):
        if ny > 1:
            for way, to in ((0, up), (1, down)):

                def make(way=way, to=to):
                    view = weights.at[rows_of(slot(y, zz, core))]
                    return view, view, sems_of(y_sem, e, way), along(to, z, core)

                send(make, cond)

    def z_send(way, hop, zz, cond):
        def inside():
            return z + 1 < nz if way == 0 else z > 0

        def wanted():
            return inside() if cond is None else jnp.logical_and(cond(), inside())

        def make():
            view = weights.at[rows_of(slot(y, zz, core))]
            to = z + 1 if way == 0 else z - 1
            return view, view, sems_of(z_sem, hop, way), along(y, to, core)

        pl.when(inside())(lambda: send(make, wanted))

    def own_weights():
        if nz > 1:
            z_send(0, 0, z, None)
            z_send(1, 0, z, None)
        y_sends(0, z, None)
        pair(0, 0, lambda: rows_of(slot(y, z, core)), None)

    def z_forward(r):
        for way in (0, 1):
            e = 1 + 2 * r + way
            zz, valid = event_of(e)

            def body(way=way, e=e, zz=zz, valid=valid):
                rows = rows_of(slot(y, zz, core))
                arrived(
                    weights.at[rows],
                    (z_sem.at[0, r, way], z_sem.at[1, r, way]),
                    along(y, zz, core),
                )
                if r + 1 < nz - 1:
                    z_send(way, r + 1, zz, valid)

            guarded(valid, body)

    def z_spread(r):
        for way in (0, 1):
            e = 1 + 2 * r + way
            zz, valid = event_of(e)

            def body(e=e, zz=zz, valid=valid):
                y_sends(e, zz, valid)
                pair(e, 0, lambda: rows_of(slot(y, zz, core)), valid)

            guarded(valid, body)

    def z_round(r):
        z_forward(r)
        z_spread(r)

    def y_first(e):
        zz, valid = event_of(e)

        def body():
            for way, origin, to in ((0, down, up), (1, up, down)):
                rows = rows_of(slot(origin, zz, core))
                arrived(
                    weights.at[rows],
                    (y_sem.at[0, e, way], y_sem.at[1, e, way]),
                    along(origin, z, core),
                )

                def make(way=way, origin=origin, to=to):
                    view = weights.at[part_of(slot(origin, zz, core), way)]
                    return view, view, sems_of(y_sem, e, 2 + way), along(to, z, core)

                send(make, valid)
                pair(e, 1 + way, lambda origin=origin: rows_of(slot(origin, zz, core)), valid)

        if ny > 1:
            guarded(valid, body)

    def y_second(e):
        zz, valid = event_of(e)

        def body():
            for way, origin in ((0, down), (1, up)):
                half = part_of(slot((y + 2) % ny, zz, core), way)
                arrived(
                    weights.at[half],
                    (y_sem.at[0, e, 2 + way], y_sem.at[1, e, 2 + way]),
                    along(origin, z, core),
                )
                pair(
                    e, 3 + way, lambda way=way: part_of(slot((y + 2) % ny, zz, core), way), valid
                )

        if ny > 1:
            guarded(valid, body)

    def pair_in(e, kinds):
        zz, valid = event_of(e)

        def body():
            other = along(y, z, 1 - core)

            def one(kind, rows):
                if kind in kinds:
                    arrived(weights.at[rows], sems_of(pair_sem, e, kind), other)

            one(0, rows_of(slot(y, zz, 1 - core)))
            if ny > 1:
                one(1, rows_of(slot(down, zz, 1 - core)))
                one(2, rows_of(slot(up, zz, 1 - core)))
                one(3, part_of(slot((y + 2) % ny, zz, 1 - core), 0))
                one(4, part_of(slot((y + 2) % ny, zz, 1 - core), 1))

        guarded(valid, body)

    events = list(range(1 + 2 * (nz - 1)))

    group_row = (group_ref[...] - ch * (width // 16)).astype(F32)
    of_group = (
        lax.broadcasted_iota(jnp.int32, (32, width), 0).astype(F32) == group_row
    ).astype(F32)
    rate_in = rate_ref[...]
    twice = 2.0 * rate_in
    series = jnp.ones_like(twice)
    for k in range(9, 1, -1):
        series = 1.0 - twice * (1.0 / k) * series
    both = jnp.concatenate([rate_in, residue_ref[...] * jnp.sqrt(twice * series)], axis=0)
    chan[...] = jnp.dot(
        both, of_group, precision=lax.Precision.HIGHEST, preferred_element_type=F32
    )

    def one_hots(joined, count):
        codes = 64 + lax.broadcasted_iota(jnp.int32, (32, count), 0)
        for back in range(3):
            shifted = joined if back == 0 else pltpu.roll(joined, back, 1)
            row = shifted[0:1, 128:]
            hot[back, 0:count] = (row == codes).astype(F32).T.astype(BF16)

    def streams(rows):
        for tile in range(width // 128):
            cols = pl.ds(tile * 128, 128)

            def mixed(i, cols=cols):
                total = None
                for back in range(3):
                    picked = jnp.dot(
                        hot[back, 0:rows], table[i, :, cols], preferred_element_type=F32
                    )
                    term = ltaps_ref[back, i : i + 1, cols] * picked
                    total = term if total is None else total + term
                return total

            key = mixed(1)
            prod[tile, 0:rows] = (key * mixed(2)).astype(BF16).astype(F32)
            query[0:rows, cols] = mixed(0)

    one_hots(jnp.concatenate([jnp.full((8, 128), -1, jnp.int32), tok_ref[...]], axis=1), tokens)
    loads[3].wait()
    loads[4].wait()
    resid[...] = jnp.dot(hot[0], emb[...], preferred_element_type=F32)
    streams(tokens)

    extra = jnp.logical_or(has_next, has_before)
    pl.semaphore_wait(barrier, len(peers) + extra.astype(jnp.int32))
    tail_tok = pl.ds(tokens - 128, 128)

    @pl.when(ctx < last_ctx)
    def _():
        send(
            lambda: (tok_ref.at[:, tail_tok], halo_tok, sems_of(tok_sem), {"ctx": ctx + 1}),
            lambda: ctx < last_ctx,
        )

    for load in loads[:3]:
        load.wait()
    own_weights()

    taps = filt_ref.shape[1]

    def make_toep(g, carry):
        line = filt_ref[pl.ds(g, 1), :]
        line = jnp.concatenate([line, jnp.zeros((1, taps), F32)], axis=1)
        spread = jnp.broadcast_to(line, (2 * taps, 2 * taps))
        turned_line = pltpu.roll(spread, taps, 1, stride=1, stride_axis=0)
        toep[g] = turned_line[:, :taps].astype(BF16)
        return carry

    lax.fori_loop(0, filt_ref.shape[0], make_toep, 0)
    lanes = lax.broadcasted_iota(jnp.int32, (128, width), 1)
    rank = jnp.zeros((1, width), F32)
    group_col = jnp.broadcast_to(group_row, (128, width)).T
    for tile in range(width // 128):
        mine = group_col[tile * 128 : (tile + 1) * 128, 0:1]
        above = tile * 128 + lax.broadcasted_iota(jnp.int32, (128, width), 0) < lanes
        same = jnp.logical_and(mine == group_row, above)
        rank = rank + jnp.sum(same.astype(F32), axis=0, keepdims=True)
    placed = group_row * float(width // 32) + rank
    for tile in range(width // 128):
        place = (tile * 128 + lax.broadcasted_iota(jnp.int32, (128, width), 0)).astype(F32)
        perm[tile * 128 : (tile + 1) * 128, :] = (place == placed).astype(F32).astype(BF16)

    @pl.when(ctx > 0)
    def _():
        arrived(halo_tok, (tok_sem.at[0], tok_sem.at[1]), {"ctx": ctx - 1})
        one_hots(jnp.concatenate([halo_tok[...], tok_ref[:, 0:128]], axis=1), 128)
        streams(16)

    chunk = tokens // 8
    chunk_id = lax.broadcasted_iota(jnp.int32, (8, 128), 0)

    def row_b(ref, p, cols):
        return jnp.broadcast_to(ref[p : p + 1, cols], (8, 128))

    for tile in range(width // 128):
        cols = pl.ds(tile * 128, 128)
        decay = [jnp.exp(-row_b(chan, p, cols)) for p in range(16)]

        def step(k, states, tile=tile, decay=decay):
            row = prod[tile, pl.ds(k, 8, stride=chunk), :]
            return tuple(d * s + row for d, s in zip(decay, states))

        states = lax.fori_loop(
            0, chunk, step, tuple(jnp.zeros((8, 128), F32) for _ in range(16)), unroll=4
        )
        for p in range(16):
            rate = row_b(chan, p, cols) * float(chunk)
            total = states[p]
            for by in (1, 2, 4):
                moved = jnp.exp(-rate * float(by)) * pltpu.roll(total, by, 0)
                total = total + jnp.where(chunk_id >= by, moved, 0.0)
            end_own[p : p + 1, cols] = total[7:8]
            excl[p, :, cols] = jnp.where(chunk_id >= 1, pltpu.roll(total, 1, 0), 0.0)

    rates = chan[0:16, :]
    send(lambda: (end_own, end_other, sems_of(end_sem), along(y, z, 1 - core)))
    arrived(end_other, (end_sem.at[0], end_sem.at[1]), along(y, z, 1 - core))
    first = jnp.where(core == 0, end_own[...], end_other[...])
    second = jnp.where(core == 0, end_other[...], end_own[...])
    decay_dev = jnp.exp(-rates * float(tokens))
    chip_own[...] = first * decay_dev + second
    for o in range(1, nz):
        send(
            lambda o=o: (
                chip_own,
                chip_all.at[z],
                (chip_sem.at[0, (z + o) % nz], chip_sem.at[1, z]),
                along(y, (z + o) % nz, core),
            )
        )
    if nz > 1:
        z_forward(0)
    y_first(0)
    for o in range(1, nz):
        origin = (z + nz - o) % nz
        arrived(
            chip_all.at[origin], (chip_sem.at[0, z], chip_sem.at[1, origin]), along(y, origin, core)
        )
    decay_chip = jnp.exp(-rates * float(2 * tokens))
    whole = None
    for zz in range(nz):
        if nz == 1:
            this = chip_own[...]
        else:
            this = jnp.where(z == zz, chip_own[...], chip_all[zz])
        whole = this if whole is None else whole * decay_chip + this
    row_own[...] = whole
    for o in range(1, ny):

        @pl.when(y + o < ny)
        def _(o=o):
            send(
                lambda: (
                    row_own,
                    row_all.at[y],
                    (row_sem.at[0, (y + o) % ny], row_sem.at[1, y]),
                    along((y + o) % ny, z, core),
                ),
                lambda: y + o < ny,
            )

    if nz > 1:
        z_spread(0)
    for o in range(1, ny):

        @pl.when(y >= o)
        def _(o=o):
            origin = (y + ny - o) % ny
            arrived(
                row_all.at[origin],
                (row_sem.at[0, y], row_sem.at[1, origin]),
                along(origin, z, core),
            )

    decay_row = jnp.exp(-rates * float(2 * tokens * nz))
    carried = jnp.zeros((16, width), F32)
    for yy in range(ny - 1):
        carried = jnp.where(yy < y, carried * decay_row + row_all[yy], carried)
    for zz in range(nz - 1):
        carried = jnp.where(zz < z, carried * decay_chip + chip_all[zz], carried)
    carried = jnp.where(core == 1, carried * decay_dev + first, carried)
    end_other[...] = carried

    for tile in range(width // 128):
        cols = pl.ds(tile * 128, 128)
        start = []
        for p in range(16):
            rate = row_b(chan, p, cols) * float(chunk)
            start.append(
                excl[p, :, cols]
                + jnp.exp(-rate * chunk_id.astype(F32)) * row_b(end_other, p, cols)
            )
        decay = [jnp.exp(-row_b(chan, p, cols)) for p in range(16)]
        weigh = [row_b(chan, 16 + p, cols) for p in range(16)]

        def step2(k, states, tile=tile, decay=decay, weigh=weigh):
            where = pl.ds(k, 8, stride=chunk)
            row = prod[tile, where, :]
            states = tuple(d * s + row for d, s in zip(decay, states))
            sums = [None] * 4
            for p in range(16):
                term = weigh[p] * states[p]
                sums[p % 4] = term if sums[p % 4] is None else sums[p % 4] + term
            conv[tile, where, :] = (sums[0] + sums[1]) + (sums[2] + sums[3])
            return states

        lax.fori_loop(0, chunk, step2, tuple(start), unroll=2)

    squares = None
    for tile in range(width // 128):
        cols = pl.ds(tile * 128, 128)
        whole = conv[tile] + lskip_ref[:, cols] * prod[tile]
        middle = (resid[:, cols] + query[:, cols] * whole).astype(BF16)
        feats[ch, :, cols] = middle
        wide = middle.astype(F32)
        resid[:, cols] = wide
        squares = wide * wide if squares is None else squares + wide * wide
    note_own[...] = jnp.broadcast_to(jnp.sum(squares.T, axis=0, keepdims=True), note_own.shape)
    note_own[1:2, :] = gain_ref[...].astype(F32)
    for o in range(1, nch):
        send(
            lambda o=o: (
                note_own,
                note_all.at[ch],
                (note_sem.at[0, (ch + o) % nch], note_sem.at[1, ch]),
                {"ch": (ch + o) % nch},
            )
        )

    right, left = (x + 1) % nx, (x + nx - 1) % nx
    far_parts = 4
    far_rows = tokens // far_parts

    def rows_x(e):
        return (0, tokens) if e == 0 else ((e - 1) * far_rows, far_rows)

    def half_x(e, way):
        base, count = rows_x(e)
        return pl.ds(base + way * (count // 2), count // 2)

    def x_sends(e):
        if nx > 1:
            for way, to in ((0, right), (1, left)):

                def make(way=way, to=to):
                    view = feats.at[side(e) * nx + x, pl.ds(*rows_x(e))]
                    return view, view, sems_of(x_sem, e, way), across(h, to)

                send(make)

    def side(e):
        return h if e == 0 else 1 - h

    def x_first(e):
        if nx > 1:
            for way, origin, to in ((0, left, right), (1, right, left)):
                block = side(e) * nx + origin
                arrived(
                    feats.at[block, pl.ds(*rows_x(e))], sems_of(x_sem, e, way), across(h, origin)
                )

                def make(way=way, block=block, to=to):
                    part = feats.at[block, half_x(e, way)]
                    return part, part, sems_of(x_sem, e, 2 + way), across(h, to)

                send(make)

    def x_second(e):
        if nx > 1:
            for way, origin in ((0, left), (1, right)):
                part = feats.at[side(e) * nx + (x + 2) % nx, half_x(e, way)]
                arrived(part, sems_of(x_sem, e, 2 + way), across(h, origin))

    def far_in(k):
        if nh > 1:
            part = feats.at[(1 - h) * nx + x, pl.ds(k * far_rows, far_rows)]
            arrived(part, sems_of(far_sem, k), across(1 - h, x))
            x_sends(1 + k)

    def x_far_first(k):
        if nh > 1:
            x_first(1 + k)

    x_sends(0)
    if nz > 2:
        z_round(1)
    if nh > 1:
        for k in range(far_parts):

            def make(k=k):
                part = feats.at[ch, pl.ds(k * far_rows, far_rows)]
                return part, part, sems_of(far_sem, k), across(1 - h, x)

            send(make)

    def y_first_if(*which):
        for e in which:
            if e in events:
                y_first(e)

    def y_second_if(*which):
        for e in which:
            if e in events:
                y_second(e)

    if nz > 3:
        z_round(2)
    x_first(0)
    y_first_if(1)
    far_in(0)
    y_first_if(2)
    far_in(1)
    y_second(0)
    y_first_if(3)
    far_in(2)
    x_far_first(0)
    y_first_if(4)
    far_in(3)
    x_far_first(1)
    y_second_if(1, 2)
    x_far_first(2)
    y_first_if(5, 6)
    x_far_first(3)

    for o in range(1, nch):
        origin = (ch + nch - o) % nch
        arrived(
            note_all.at[origin], (note_sem.at[0, ch], note_sem.at[1, origin]), {"ch": origin}
        )
    note_all[ch] = note_own[...]
    total = note_all[0, 0:1, :]
    for o in range(1, nch):
        total = total + note_all[o, 0:1, :]
    factor = lax.rsqrt(total / float(width * nch) + EPSILON)
    scale[...] = jnp.broadcast_to(factor, (128, tokens)).T

    per_tile = 256
    per_row = nch // ny

    def block_product(block):
        gain = note_all[block, 1:2, :]
        for tile in range(width // 128):
            cols = pl.ds(tile * 128, 128)
            wide = feats[block, :, cols].astype(F32) * scale[...]
            half_norm[:, cols] = (wide * gain[:, tile * 128 : (tile + 1) * 128]).astype(BF16)
        rows = pl.ds(pl.multiple_of(block * width, width), width)

        def columns(j, inner):
            cols = pl.ds(pl.multiple_of(j * per_tile, per_tile), per_tile)
            made = jnp.dot(half_norm[...], weights[rows, cols], preferred_element_type=F32)
            acc[HALO:, cols] += made
            return inner

        lax.fori_loop(0, acc.shape[1] // per_tile, columns, 0)

    def early(block):
        same = block // nx == h
        return same if per_row == 0 else jnp.logical_and(same, block // per_row != (y + 2) % ny)

    def product_if(wanted):
        def body(block, carry):
            @pl.when(wanted(block))
            def _():
                block_product(block)

            return carry

        lax.fori_loop(0, nch, body, 0)

    acc[...] = jnp.zeros_like(acc)
    x_second(0)
    for e in events:
        pair_in(e, (0, 1, 2))
    y_second_if(3, 4)
    if per_row > 0 and ny > 1:
        product_if(early)
    elif ny == 1:
        product_if(lambda block: block // nx == h)
    y_second_if(5, 6)
    if nh > 1:
        for k in range(far_parts):
            x_second(1 + k)
    for e in events:
        pair_in(e, (3, 4))
    if per_row > 0 and ny > 1:
        product_if(lambda block: jnp.logical_not(early(block)))
    elif ny == 1:
        product_if(lambda block: block // nx != h)
    else:
        block_product(0)

    for tile in range(acc.shape[1] // 256):
        cols = pl.ds(tile * 256, 256)
        last = acc[tokens:, cols].astype(BF16)
        tail_out[:, cols] = last
        acc[tokens:, cols] = last.astype(F32)

    @pl.when(ctx < last_ctx)
    def _():
        send(
            lambda: (tail_out, tail_in, sems_of(tail_sem), {"ctx": ctx + 1}),
            lambda: ctx < last_ctx,
        )

    for tile in range(acc.shape[1] // 256):
        cols = pl.ds(tile * 256, 256)
        acc[HALO:tokens, cols] = acc[HALO:tokens, cols].astype(BF16).astype(F32)

    @pl.when(ctx > 0)
    def _():
        arrived(tail_in, (tail_sem.at[0], tail_sem.at[1]), {"ctx": ctx - 1})
        acc[0:HALO, :] = tail_in[...].astype(F32)

    def mixed2(i, base, count, tile):
        cols = pl.ds(i * width + tile * 128, 128)
        at = pl.ds(tile * 128, 128)
        total = None
        for back in range(3):
            term = (
                mtaps_ref[back, i : i + 1, at]
                * acc[base - back : base - back + count, cols]
            )
            total = term if total is None else total + term
        return total

    for tile in range(width // 128):
        cols = pl.ds(tile * 128, 128)
        for base in range(HALO - 128, HALO + tokens, 128):
            made = mixed2(1, base, 128, tile) * mixed2(2, base, 128, tile)
            prod2[base - HALO + 128 : base - HALO + 256, cols] = made.astype(BF16)
            if base >= HALO:
                query[base - HALO : base - HALO + 128, cols] = mixed2(0, base, 128, tile)
    for tile in range(width // 128):
        lines = pl.ds(tile * 128, 128)
        made = lax.dot_general(
            perm[lines, :], prod2[...], (((1,), (1,)), ((), ())), preferred_element_type=F32
        )
        turned[lines, :] = made.astype(BF16)

    members = width // 32

    def one_group(g, carry):
        lines = pl.ds(pl.multiple_of(g * members, members), members)
        data = jnp.concatenate(
            [turned[lines, n * 128 : n * 128 + 256] for n in range(tokens // 128)], axis=0
        )
        made = jnp.dot(data, toep[g], preferred_element_type=F32)
        upper = made.astype(BF16)
        lower = (made - upper.astype(F32)).astype(BF16)
        for n in range(tokens // 128):
            conv_hi[lines, n * 128 : (n + 1) * 128] = upper[n * members : (n + 1) * members]
            conv_lo[lines, n * 128 : (n + 1) * 128] = lower[n * members : (n + 1) * members]
        return carry

    lax.fori_loop(0, 32, one_group, 0)
    flip = (((0,), (0,)), ((), ()))
    for tile in range(width // 256):
        cols = pl.ds(tile * 256, 256)
        made = lax.dot_general(conv_hi[...], perm[:, cols], flip, preferred_element_type=F32)
        made = made + lax.dot_general(
            conv_lo[...], perm[:, cols], flip, preferred_element_type=F32
        )
        made = made + mskip_ref[:, cols] * prod2[128:, cols].astype(F32)
        out_ref[:, cols] = (resid[:, cols] + query[:, cols] * made).astype(BF16)

    for make, cond in waits:
        if cond is None:
            copy(*make()).wait_send()
        else:
            pl.when(cond())(lambda make=make: copy(*make()).wait_send())


def local(sizes, *arrays):
    (
        token_ids,
        embedding,
        long_table,
        long_taps,
        long_residue,
        long_rate,
        long_skip,
        medium_gain,
        medium_weight,
        medium_taps,
        medium_group_filter,
        medium_skip,
        filter_group,
    ) = arrays
    ny, nz, nh, nx = sizes
    nch, nctx = nh * nx, 2 * ny * nz
    tokens, width = token_ids.shape[0], embedding.shape[1]
    piece = medium_weight.shape[0]
    events = 1 + 2 * (nz - 1)
    hops = max(nz - 1, 1)
    vmem = pl.BlockSpec(memory_space=pltpu.VMEM)
    hbm = pl.BlockSpec(memory_space=pl.ANY)
    dma = pltpu.SemaphoreType.DMA
    return pl.pallas_call(
        functools.partial(kernel, sizes),
        out_shape=jax.ShapeDtypeStruct((tokens, width), BF16),
        in_specs=[vmem, hbm, hbm] + [vmem] * 5 + [hbm] + [vmem] * 4,
        out_specs=vmem,
        scratch_shapes=[
            pltpu.VMEM((32, width), BF16),
            pltpu.VMEM((3, 32, width), BF16),
            pltpu.VMEM((8, tokens), jnp.int32),
            pltpu.VMEM((nctx * piece, 3 * width), BF16),
            pltpu.VMEM((nch, tokens, width), BF16),
            pltpu.VMEM((HALO + tokens, 3 * width), F32),
            pltpu.VMEM((3, tokens, 32), BF16),
            pltpu.VMEM((8, 128), jnp.int32),
            pltpu.VMEM((width // 128, tokens, 128), F32),
            pltpu.VMEM((tokens, width), F32),
            pltpu.VMEM((tokens, width), F32),
            pltpu.VMEM((width // 128, tokens, 128), F32),
            pltpu.VMEM((32, width), F32),
            pltpu.VMEM((16, 8, width), F32),
            pltpu.VMEM((16, width), F32),
            pltpu.VMEM((16, width), F32),
            pltpu.VMEM((16, width), F32),
            pltpu.VMEM((nz, 16, width), F32),
            pltpu.VMEM((16, width), F32),
            pltpu.VMEM((ny, 16, width), F32),
            pltpu.VMEM((8, tokens), F32),
            pltpu.VMEM((nch, 8, tokens), F32),
            pltpu.VMEM((tokens, 128), F32),
            pltpu.VMEM((tokens, width), BF16),
            pltpu.VMEM((width, width), BF16),
            pltpu.VMEM((32, 256, 128), BF16),
            pltpu.VMEM((HALO, 3 * width), BF16),
            pltpu.VMEM((HALO, 3 * width), BF16),
            pltpu.VMEM((128 + tokens, width), BF16),
            pltpu.VMEM((width, 128 + tokens), BF16),
            pltpu.VMEM((width, tokens), BF16),
            pltpu.VMEM((width, tokens), BF16),
            dma((5,)),
            dma((2,)),
            dma((2, hops, 2)),
            dma((2, events, 4)),
            dma((2, events, 5)),
            dma((2,)),
            dma((2, nz)),
            dma((2, ny)),
            dma((2, nch)),
            dma((2, 5, 4)),
            dma((2, 4)),
            dma((2,)),
        ],
        compiler_params=pltpu.CompilerParams(
            collective_id=0, has_side_effects=True, vmem_limit_bytes=60 << 20
        ),
    )(
        token_ids[None],
        embedding,
        jnp.transpose(long_table, (1, 0, 2)),
        long_taps,
        long_residue.T,
        long_rate.T,
        long_skip[None],
        medium_gain[None],
        jnp.transpose(medium_weight, (1, 0, 2)),
        medium_taps,
        medium_group_filter,
        medium_skip[None],
        filter_group[None],
    )


def solution(mesh, sizes=(4, 4, 2, 4)):
    in_specs = (
        P("ctx"),
        P(None, "ch"),
        P(None, None, "ch"),
        P(None, None, "ch"),
        P("ch", None),
        P("ch", None),
        P("ch"),
        P("ch"),
        P("ctx", None, "ch"),
        P(None, None, "ch"),
        P("ch", None),
        P("ch"),
        P("ch"),
    )
    return jax.shard_map(
        functools.partial(local, sizes),
        mesh=mesh,
        in_specs=in_specs,
        out_specs=P("ctx", "ch"),
        check_vma=False,
    )
```

time: 568 us -> 116 us (0.20)
  the two profiles are of different devices: /device:TPU:49 before, /device:TPU:8 now
where the time goes in v1:
time: 116 us; the launch traced here: 115 us
  Pallas kernels  112 us (97%)
  local copies, waits for them, and re-layouts  3.13 us (3%)
    pallas_call x1, Pallas kernels, local(): pl.pallas_call(functools.partial(kernel, sizes), out_shape=jax.ShapeDtype...  112 us

profile of v1, /device:TPU:8, one launch (start us, length us, event | category | flops | bytes accessed | tf_op | source)
XLA Modules:
  0.0 115.4 jit_solution(12345831078909157572)
XLA Ops:
  0.0 1.3 %broadcast_in_dim.17.gain_ref = bf16[1,512]{1,0:T(2,128)(2,1)} reshape(bf16[512]{0:T(512)(128)(2,1)} %param.20) | data formatting | bytes 2048 | tf_op jit(solution)/shard_map/broadcast_in_dim | solution.py:866
  1.3 112.3 %shard_map.127 = bf16[512,512]{1,0:T(8,128)(2,1)} custom-call(s32[1,512]{1,0:T(1,128)} %bitcast.12, bf16[512,512]{1,0:T(8,128)(2,1)} %emb_ref.1, bf16[3,512,512]{2,1,0:T(8,128)(2,1)} %bitcast.8, f32[3,3,512]{2,1,0:T(4,128)} %ltaps_ref.1, f32[16,32]{1,0:T(8,128)} %bitcast.10, f32[16,32]{1,0:T(8,128)} %bitcast.11, f32[1,512]{1,0:T(1,128)} %bitcast.13, ...), custom_call_target="tpu_custom_call" | custom-call | tf_op jit(solution)/shard_map/pallas_call | solution.py:804
  113.5 1.9 %copy.15 = bf16[512,512]{1,0:T(8,128)(2,1)} copy(bf16[512,512]{1,0:T(8,128)(2,1)} %shard_map.127) | data formatting | bytes 1048576

commit v2 on v1

--- a/solution.py
+++ b/solution.py
@@ -588,8 +588,8 @@
             x_first(1 + k)
 
     x_sends(0)
-    if nz > 2:
-        z_round(1)
+    for r in range(1, nz - 1):
+        z_round(r)
     if nh > 1:
         for k in range(far_parts):
 
@@ -609,24 +609,18 @@
             if e in events:
                 y_second(e)
 
-    if nz > 3:
-        z_round(2)
+    acc[...] = jnp.zeros_like(acc)
     x_first(0)
-    y_first_if(1)
+    y_first_if(1, 2)
+    y_second(0)
     far_in(0)
-    y_first_if(2)
     far_in(1)
-    y_second(0)
-    y_first_if(3)
+    x_far_first(0)
+    y_first_if(3, 4)
     far_in(2)
-    x_far_first(0)
-    y_first_if(4)
+    x_far_first(1)
     far_in(3)
-    x_far_first(1)
-    y_second_if(1, 2)
-    x_far_first(2)
     y_first_if(5, 6)
-    x_far_first(3)
 
     for o in range(1, nch):
         origin = (ch + nch - o) % nch
@@ -642,80 +636,97 @@
 
     per_tile = 256
     per_row = nch // ny
-
-    def block_product(block):
+    wide_all = acc.shape[1]
+
+    def block_product(block, top, count):
         gain = note_all[block, 1:2, :]
         for tile in range(width // 128):
             cols = pl.ds(tile * 128, 128)
-            wide = feats[block, :, cols].astype(F32) * scale[...]
-            half_norm[:, cols] = (wide * gain[:, tile * 128 : (tile + 1) * 128]).astype(BF16)
+            wide = feats[block, top : top + count, cols].astype(F32) * scale[top : top + count, :]
+            half_norm[top : top + count, cols] = (
+                wide * gain[:, tile * 128 : (tile + 1) * 128]
+            ).astype(BF16)
         rows = pl.ds(pl.multiple_of(block * width, width), width)
-
-        def columns(j, inner):
-            cols = pl.ds(pl.multiple_of(j * per_tile, per_tile), per_tile)
-            made = jnp.dot(half_norm[...], weights[rows, cols], preferred_element_type=F32)
-            acc[HALO:, cols] += made
-            return inner
-
-        lax.fori_loop(0, acc.shape[1] // per_tile, columns, 0)
+        for tile in range(wide_all // per_tile):
+            cols = pl.ds(tile * per_tile, per_tile)
+            acc[HALO + top : HALO + top + count, cols] += jnp.dot(
+                half_norm[top : top + count, :], weights[rows, cols], preferred_element_type=F32
+            )
 
     def early(block):
         same = block // nx == h
-        return same if per_row == 0 else jnp.logical_and(same, block // per_row != (y + 2) % ny)
-
-    def product_if(wanted):
-        def body(block, carry):
+        if ny == 1:
+            return same
+        return jnp.logical_and(same, block // per_row != (y + 2) % ny)
+
+    def late(block):
+        return jnp.logical_not(early(block))
+
+    def product_if(wanted, first, count, top, rows):
+        def body(i, carry):
+            block = first + i
+
             @pl.when(wanted(block))
             def _():
-                block_product(block)
+                block_product(block, top, rows)
 
             return carry
 
-        lax.fori_loop(0, nch, body, 0)
-
-    acc[...] = jnp.zeros_like(acc)
+        lax.fori_loop(0, count, body, 0)
+
+    split = nch > 1
     x_second(0)
     for e in events:
         pair_in(e, (0, 1, 2))
-    y_second_if(3, 4)
-    if per_row > 0 and ny > 1:
-        product_if(early)
-    elif ny == 1:
-        product_if(lambda block: block // nx == h)
-    y_second_if(5, 6)
+    x_far_first(2)
+    if split:
+        product_if(early, h * nx, nx // 2, 0, tokens)
+    x_far_first(3)
+    y_second_if(1, 2)
+    if split:
+        product_if(early, h * nx + nx // 2, nx // 2, 0, tokens)
+    y_second_if(3, 4, 5, 6)
     if nh > 1:
         for k in range(far_parts):
             x_second(1 + k)
     for e in events:
         pair_in(e, (3, 4))
-    if per_row > 0 and ny > 1:
-        product_if(lambda block: jnp.logical_not(early(block)))
-    elif ny == 1:
-        product_if(lambda block: block // nx != h)
+
+    body_rows = tokens - HALO
+    if split:
+        product_if(late, 0, nch, body_rows, HALO)
     else:
-        block_product(0)
-
-    for tile in range(acc.shape[1] // 256):
+        block_product(0, body_rows, HALO)
+    for tile in range(wide_all // 256):
         cols = pl.ds(tile * 256, 256)
         last = acc[tokens:, cols].astype(BF16)
         tail_out[:, cols] = last
         acc[tokens:, cols] = last.astype(F32)
+    tail_parts = (
+        (pl.ds(0, HALO), pl.ds(width, 2 * width)),
+        (pl.ds(HALO - 16, 16), pl.ds(0, width)),
+    )
 
     @pl.when(ctx < last_ctx)
     def _():
-        send(
-            lambda: (tail_out, tail_in, sems_of(tail_sem), {"ctx": ctx + 1}),
-            lambda: ctx < last_ctx,
-        )
-
-    for tile in range(acc.shape[1] // 256):
+        for k, part in enumerate(tail_parts):
+            send(
+                lambda k=k, part=part: (
+                    tail_out.at[part],
+                    tail_in.at[part],
+                    sems_of(tail_sem, k),
+                    {"ctx": ctx + 1},
+                ),
+                lambda: ctx < last_ctx,
+            )
+
+    if split:
+        product_if(late, 0, nch, 0, body_rows)
+    else:
+        block_product(0, 0, body_rows)
+    for tile in range(wide_all // 256):
         cols = pl.ds(tile * 256, 256)
         acc[HALO:tokens, cols] = acc[HALO:tokens, cols].astype(BF16).astype(F32)
-
-    @pl.when(ctx > 0)
-    def _():
-        arrived(tail_in, (tail_sem.at[0], tail_sem.at[1]), {"ctx": ctx - 1})
-        acc[0:HALO, :] = tail_in[...].astype(F32)
 
     def mixed2(i, base, count, tile):
         cols = pl.ds(i * width + tile * 128, 128)
@@ -729,51 +740,74 @@
             total = term if total is None else total + term
         return total
 
-    for tile in range(width // 128):
-        cols = pl.ds(tile * 128, 128)
-        for base in range(HALO - 128, HALO + tokens, 128):
-            made = mixed2(1, base, 128, tile) * mixed2(2, base, 128, tile)
-            prod2[base - HALO + 128 : base - HALO + 256, cols] = made.astype(BF16)
-            if base >= HALO:
-                query[base - HALO : base - HALO + 128, cols] = mixed2(0, base, 128, tile)
-    for tile in range(width // 128):
-        lines = pl.ds(tile * 128, 128)
-        made = lax.dot_general(
-            perm[lines, :], prod2[...], (((1,), (1,)), ((), ())), preferred_element_type=F32
-        )
-        turned[lines, :] = made.astype(BF16)
-
     members = width // 32
-
-    def one_group(g, carry):
-        lines = pl.ds(pl.multiple_of(g * members, members), members)
-        data = jnp.concatenate(
-            [turned[lines, n * 128 : n * 128 + 256] for n in range(tokens // 128)], axis=0
-        )
-        made = jnp.dot(data, toep[g], preferred_element_type=F32)
-        upper = made.astype(BF16)
-        lower = (made - upper.astype(F32)).astype(BF16)
-        for n in range(tokens // 128):
-            conv_hi[lines, n * 128 : (n + 1) * 128] = upper[n * members : (n + 1) * members]
-            conv_lo[lines, n * 128 : (n + 1) * 128] = lower[n * members : (n + 1) * members]
-        return carry
-
-    lax.fori_loop(0, 32, one_group, 0)
     flip = (((0,), (0,)), ((), ()))
-    for tile in range(width // 256):
-        cols = pl.ds(tile * 256, 256)
-        made = lax.dot_general(conv_hi[...], perm[:, cols], flip, preferred_element_type=F32)
-        made = made + lax.dot_general(
-            conv_lo[...], perm[:, cols], flip, preferred_element_type=F32
-        )
-        made = made + mskip_ref[:, cols] * prod2[128:, cols].astype(F32)
-        out_ref[:, cols] = (resid[:, cols] + query[:, cols] * made).astype(BF16)
-
+
+    def products(bases):
+        for tile in range(width // 128):
+            cols = pl.ds(tile * 128, 128)
+            for base in bases:
+                made = mixed2(1, base, 128, tile) * mixed2(2, base, 128, tile)
+                prod2[base - HALO + 128 : base - HALO + 256, cols] = made.astype(BF16)
+                if base >= HALO:
+                    query[base - HALO : base - HALO + 128, cols] = mixed2(0, base, 128, tile)
+        top, end = bases[0] - HALO + 128, bases[-1] - HALO + 256
+        for tile in range(width // 128):
+            lines = pl.ds(tile * 128, 128)
+            made = lax.dot_general(
+                perm[lines, :],
+                prod2[top:end, :],
+                (((1,), (1,)), ((), ())),
+                preferred_element_type=F32,
+            )
+            turned[lines, top:end] = made.astype(BF16)
+
+    def filtered(blocks):
+        def one_group(g, carry):
+            lines = pl.ds(pl.multiple_of(g * members, members), members)
+            data = jnp.concatenate(
+                [turned[lines, n * 128 : n * 128 + 256] for n in blocks], axis=0
+            )
+            made = jnp.dot(data, toep[g], preferred_element_type=F32)
+            upper = made.astype(BF16)
+            lower = (made - upper.astype(F32)).astype(BF16)
+            for k, n in enumerate(blocks):
+                conv_hi[lines, n * 128 : (n + 1) * 128] = upper[k * members : (k + 1) * members]
+                conv_lo[lines, n * 128 : (n + 1) * 128] = lower[k * members : (k + 1) * members]
+            return carry
+
+        lax.fori_loop(0, 32, one_group, 0, unroll=4)
+        top, end = blocks[0] * 128, (blocks[-1] + 1) * 128
+        for tile in range(width // 256):
+            cols = pl.ds(tile * 256, 256)
+            made = lax.dot_general(
+                conv_hi[:, top:end], perm[:, cols], flip, preferred_element_type=F32
+            )
+            made = made + lax.dot_general(
+                conv_lo[:, top:end], perm[:, cols], flip, preferred_element_type=F32
+            )
+            made = made + mskip_ref[:, cols] * prod2[128 + top : 128 + end, cols].astype(F32)
+            out_ref[top:end, cols] = (
+                resid[top:end, cols] + query[top:end, cols] * made
+            ).astype(BF16)
+
+    products([HALO + 128, HALO + 256, HALO + 384])
+    filtered((2, 3))
     for make, cond in waits:
         if cond is None:
             copy(*make()).wait_send()
         else:
             pl.when(cond())(lambda make=make: copy(*make()).wait_send())
+
+    @pl.when(ctx > 0)
+    def _():
+        for k, part in enumerate(tail_parts):
+            arrived(tail_in.at[part], sems_of(tail_sem, k), {"ctx": ctx - 1})
+        acc[0:HALO, width:] = tail_in[:, width:].astype(F32)
+        acc[HALO - 16 : HALO, 0:width] = tail_in[HALO - 16 :, 0:width].astype(F32)
+
+    products([HALO - 128, HALO])
+    filtered((0, 1))
 
 
 def local(sizes, *arrays):
@@ -850,7 +884,7 @@
             dma((2, nch)),
             dma((2, 5, 4)),
             dma((2, 4)),
-            dma((2,)),
+            dma((2, 2)),
         ],
         compiler_params=pltpu.CompilerParams(
             collective_id=0, has_side_effects=True, vmem_limit_bytes=60 << 20

time: 116 us -> 101 us (0.87)
  the two profiles are of different devices: /device:TPU:8 before, /device:TPU:19 now
where the time goes in v2:
time: 101 us
  Pallas kernels  98 us (97%)
  local copies, waits for them, and re-layouts  3.13 us (3%)
    pallas_call x1, Pallas kernels, local(): pl.pallas_call(functools.partial(kernel, sizes), out_shape=jax.ShapeDtype...  98 us

profile of v2, /device:TPU:19, one launch (start us, length us, event | category | flops | bytes accessed | tf_op | source)
XLA Modules:
  0.0 101.2 jit_solution(2503502842135621458)
XLA Ops:
  0.0 1.3 %broadcast_in_dim.17.gain_ref = bf16[1,512]{1,0:T(2,128)(2,1)} reshape(bf16[512]{0:T(512)(128)(2,1)} %param.20) | data formatting | bytes 2048 | tf_op jit(solution)/shard_map/broadcast_in_dim | solution.py:900
  1.3 98.0 %shard_map.127 = bf16[512,512]{1,0:T(8,128)(2,1)} custom-call(s32[1,512]{1,0:T(1,128)} %bitcast.12, bf16[512,512]{1,0:T(8,128)(2,1)} %emb_ref.1, bf16[3,512,512]{2,1,0:T(8,128)(2,1)} %bitcast.8, f32[3,3,512]{2,1,0:T(4,128)} %ltaps_ref.1, f32[16,32]{1,0:T(8,128)} %bitcast.10, f32[16,32]{1,0:T(8,128)} %bitcast.11, f32[1,512]{1,0:T(1,128)} %bitcast.13, ...), custom_call_target="tpu_custom_call" | custom-call | tf_op jit(solution)/shard_map/pallas_call | solution.py:838
  99.3 1.9 %copy.15 = bf16[512,512]{1,0:T(8,128)(2,1)} copy(bf16[512,512]{1,0:T(8,128)(2,1)} %shard_map.127) | data formatting | bytes 1048576

commit v3 on v2

--- a/solution.py
+++ b/solution.py
@@ -28,6 +28,7 @@
     filt_ref,
     mskip_ref,
     group_ref,
+    out_hbm,
     out_ref,
     emb,
     table,
@@ -73,6 +74,7 @@
     x_sem,
     far_sem,
     tail_sem,
+    out_sem,
 ):
     ny, nz, nh, nx = sizes
     nch = nh * nx
@@ -417,6 +419,26 @@
                 total = total + jnp.where(chunk_id >= by, moved, 0.0)
             end_own[p : p + 1, cols] = total[7:8]
             excl[p, :, cols] = jnp.where(chunk_id >= 1, pltpu.roll(total, 1, 0), 0.0)
+
+    def own_conv(tiles):
+        for tile in tiles:
+            cols = pl.ds(tile * 128, 128)
+            decay = [jnp.exp(-row_b(chan, p, cols)) for p in range(16)]
+            weigh = [row_b(chan, 16 + p, cols) for p in range(16)]
+
+            def step2(k, states, tile=tile, decay=decay, weigh=weigh):
+                where = pl.ds(k, 8, stride=chunk)
+                row = prod[tile, where, :]
+                states = tuple(d * s + row for d, s in zip(decay, states))
+                sums = [None] * 4
+                for p in range(16):
+                    term = weigh[p] * states[p]
+                    sums[p % 4] = term if sums[p % 4] is None else sums[p % 4] + term
+                conv[tile, where, :] = (sums[0] + sums[1]) + (sums[2] + sums[3])
+                return states
+
+            start = tuple(excl[p, :, cols] for p in range(16))
+            lax.fori_loop(0, chunk, step2, start, unroll=2)
 
     rates = chan[0:16, :]
     send(lambda: (end_own, end_other, sems_of(end_sem), along(y, z, 1 - core)))
@@ -434,9 +456,9 @@
                 along(y, (z + o) % nz, core),
             )
         )
+    own_conv((0, 1))
     if nz > 1:
         z_forward(0)
-    y_first(0)
     for o in range(1, nz):
         origin = (z + nz - o) % nz
         arrived(
@@ -467,6 +489,8 @@
 
     if nz > 1:
         z_spread(0)
+    y_first(0)
+    own_conv((2, 3))
     for o in range(1, ny):
 
         @pl.when(y >= o)
@@ -491,26 +515,20 @@
         cols = pl.ds(tile * 128, 128)
         start = []
         for p in range(16):
-            rate = row_b(chan, p, cols) * float(chunk)
-            start.append(
-                excl[p, :, cols]
-                + jnp.exp(-rate * chunk_id.astype(F32)) * row_b(end_other, p, cols)
-            )
+            rate = row_b(chan, p, cols)
+            since = rate * (chunk_id * chunk + 1).astype(F32)
+            start.append(row_b(chan, 16 + p, cols) * row_b(end_other, p, cols) * jnp.exp(-since))
         decay = [jnp.exp(-row_b(chan, p, cols)) for p in range(16)]
-        weigh = [row_b(chan, 16 + p, cols) for p in range(16)]
-
-        def step2(k, states, tile=tile, decay=decay, weigh=weigh):
+
+        def step3(k, states, tile=tile, decay=decay):
             where = pl.ds(k, 8, stride=chunk)
-            row = prod[tile, where, :]
-            states = tuple(d * s + row for d, s in zip(decay, states))
-            sums = [None] * 4
-            for p in range(16):
-                term = weigh[p] * states[p]
-                sums[p % 4] = term if sums[p % 4] is None else sums[p % 4] + term
-            conv[tile, where, :] = (sums[0] + sums[1]) + (sums[2] + sums[3])
-            return states
-
-        lax.fori_loop(0, chunk, step2, tuple(start), unroll=2)
+            sums = list(states[:4])
+            for p in range(4, 16):
+                sums[p % 4] = sums[p % 4] + states[p]
+            conv[tile, where, :] += (sums[0] + sums[1]) + (sums[2] + sums[3])
+            return tuple(d * s for d, s in zip(decay, states))
+
+        lax.fori_loop(0, chunk, step3, tuple(start), unroll=4)
 
     squares = None
     for tile in range(width // 128):
@@ -588,16 +606,18 @@
             x_first(1 + k)
 
     x_sends(0)
-    for r in range(1, nz - 1):
-        z_round(r)
-    if nh > 1:
-        for k in range(far_parts):
-
-            def make(k=k):
-                part = feats.at[ch, pl.ds(k * far_rows, far_rows)]
-                return part, part, sems_of(far_sem, k), across(1 - h, x)
-
-            send(make)
+    def far_out(*which):
+        if nh > 1:
+            for k in which:
+
+                def make(k=k):
+                    part = feats.at[ch, pl.ds(k * far_rows, far_rows)]
+                    return part, part, sems_of(far_sem, k), across(1 - h, x)
+
+                send(make)
+
+    if nz > 2:
+        z_round(1)
 
     def y_first_if(*which):
         for e in which:
@@ -610,13 +630,17 @@
                 y_second(e)
 
     acc[...] = jnp.zeros_like(acc)
+    y_first_if(1)
     x_first(0)
-    y_first_if(1, 2)
-    y_second(0)
+    if nz > 3:
+        z_round(2)
+    far_out(*range(far_parts))
+    y_first_if(2)
     far_in(0)
+    y_first_if(3, 4)
     far_in(1)
     x_far_first(0)
-    y_first_if(3, 4)
+    y_second(0)
     far_in(2)
     x_far_first(1)
     far_in(3)
@@ -676,9 +700,9 @@
 
     split = nch > 1
     x_second(0)
+    x_far_first(2)
     for e in events:
         pair_in(e, (0, 1, 2))
-    x_far_first(2)
     if split:
         product_if(early, h * nx, nx // 2, 0, tokens)
     x_far_first(3)
@@ -791,8 +815,13 @@
                 resid[top:end, cols] + query[top:end, cols] * made
             ).astype(BF16)
 
+    def put(part):
+        rows = pl.ds(part * (tokens // 2), tokens // 2)
+        return pltpu.make_async_copy(out_ref.at[rows], out_hbm.at[rows], out_sem.at[part])
+
     products([HALO + 128, HALO + 256, HALO + 384])
     filtered((2, 3))
+    put(1).start()
     for make, cond in waits:
         if cond is None:
             copy(*make()).wait_send()
@@ -808,6 +837,9 @@
 
     products([HALO - 128, HALO])
     filtered((0, 1))
+    put(0).start()
+    put(0).wait()
+    put(1).wait()
 
 
 def local(sizes, *arrays):
@@ -839,8 +871,9 @@
         functools.partial(kernel, sizes),
         out_shape=jax.ShapeDtypeStruct((tokens, width), BF16),
         in_specs=[vmem, hbm, hbm] + [vmem] * 5 + [hbm] + [vmem] * 4,
-        out_specs=vmem,
+        out_specs=hbm,
         scratch_shapes=[
+            pltpu.VMEM((tokens, width), BF16),
             pltpu.VMEM((32, width), BF16),
             pltpu.VMEM((3, 32, width), BF16),
             pltpu.VMEM((8, tokens), jnp.int32),
@@ -885,6 +918,7 @@
             dma((2, 5, 4)),
             dma((2, 4)),
             dma((2, 2)),
+            dma((2,)),
         ],
         compiler_params=pltpu.CompilerParams(
             collective_id=0, has_side_effects=True, vmem_limit_bytes=60 << 20

time: 101 us -> 97.6 us (0.966)
  the two profiles are of different devices: /device:TPU:19 before, /device:TPU:49 now
where the time goes in v3:
time: 97.6 us; the launch traced here: 97.4 us
  Pallas kernels  94.2 us (97%)
  local copies, waits for them, and re-layouts  3.13 us (3%)
    pallas_call x1, Pallas kernels, local(): pl.pallas_call(functools.partial(kernel, sizes), out_shape=jax.ShapeDtype...  94.2 us

profile of v3, /device:TPU:49, one launch (start us, length us, event | category | flops | bytes accessed | tf_op | source)
XLA Modules:
  0.0 97.4 jit_solution(4460349543079851223)
XLA Ops:
  0.0 1.3 %broadcast_in_dim.17.gain_ref = bf16[1,512]{1,0:T(2,128)(2,1)} reshape(bf16[512]{0:T(512)(128)(2,1)} %param.20) | data formatting | bytes 2048 | tf_op jit(solution)/shard_map/broadcast_in_dim | solution.py:934
  1.3 94.2 %shard_map.127 = bf16[512,512]{1,0:T(8,128)(2,1)} custom-call(s32[1,512]{1,0:T(1,128)} %bitcast.12, bf16[512,512]{1,0:T(8,128)(2,1)} %emb_ref.1, bf16[3,512,512]{2,1,0:T(8,128)(2,1)} %bitcast.8, f32[3,3,512]{2,1,0:T(4,128)} %ltaps_ref.1, f32[16,32]{1,0:T(8,128)} %bitcast.10, f32[16,32]{1,0:T(8,128)} %bitcast.11, f32[1,512]{1,0:T(1,128)} %bitcast.13, ...), custom_call_target="tpu_custom_call" | custom-call | tf_op jit(solution)/shard_map/pallas_call | solution.py:870
  95.5 1.9 %copy.15 = bf16[512,512]{1,0:T(8,128)(2,1)} copy(bf16[512,512]{1,0:T(8,128)(2,1)} %shard_map.127) | data formatting | bytes 1048576

commit v4 on v3

--- a/solution.py
+++ b/solution.py
@@ -61,7 +61,6 @@
     prod2,
     turned,
     conv_hi,
-    conv_lo,
     load_sem,
     tok_sem,
     z_sem,
@@ -176,7 +175,7 @@
     def pair(e, kind, rows, cond):
         def make():
             view = weights.at[rows()]
-            return view, view, sems_of(pair_sem, e, kind), along(y, z, 1 - core)
+            return view, view, sems_of(pair_sem, event_of(e)[0], kind), along(y, z, 1 - core)
 
         send(make, cond)
 
@@ -186,7 +185,7 @@
 
                 def make(way=way, to=to):
                     view = weights.at[rows_of(slot(y, zz, core))]
-                    return view, view, sems_of(y_sem, e, way), along(to, z, core)
+                    return view, view, sems_of(y_sem, zz, way), along(to, z, core)
 
                 send(make, cond)
 
@@ -251,13 +250,13 @@
                 rows = rows_of(slot(origin, zz, core))
                 arrived(
                     weights.at[rows],
-                    (y_sem.at[0, e, way], y_sem.at[1, e, way]),
+                    sems_of(y_sem, zz, way),
                     along(origin, z, core),
                 )
 
                 def make(way=way, origin=origin, to=to):
                     view = weights.at[part_of(slot(origin, zz, core), way)]
-                    return view, view, sems_of(y_sem, e, 2 + way), along(to, z, core)
+                    return view, view, sems_of(y_sem, zz, 2 + way), along(to, z, core)
 
                 send(make, valid)
                 pair(e, 1 + way, lambda origin=origin: rows_of(slot(origin, zz, core)), valid)
@@ -273,7 +272,7 @@
                 half = part_of(slot((y + 2) % ny, zz, core), way)
                 arrived(
                     weights.at[half],
-                    (y_sem.at[0, e, 2 + way], y_sem.at[1, e, 2 + way]),
+                    sems_of(y_sem, zz, 2 + way),
                     along(origin, z, core),
                 )
                 pair(
@@ -291,7 +290,7 @@
 
             def one(kind, rows):
                 if kind in kinds:
-                    arrived(weights.at[rows], sems_of(pair_sem, e, kind), other)
+                    arrived(weights.at[rows], sems_of(pair_sem, zz, kind), other)
 
             one(0, rows_of(slot(y, zz, 1 - core)))
             if ny > 1:
@@ -689,11 +688,10 @@
     def product_if(wanted, first, count, top, rows):
         def body(i, carry):
             block = first + i
-
-            @pl.when(wanted(block))
-            def _():
+            if wanted is None:
                 block_product(block, top, rows)
-
+            else:
+                pl.when(wanted(block))(lambda: block_product(block, top, rows))
             return carry
 
         lax.fori_loop(0, count, body, 0)
@@ -701,24 +699,26 @@
     split = nch > 1
     x_second(0)
     x_far_first(2)
+    y_second_if(1, 2, 3, 4)
     for e in events:
         pair_in(e, (0, 1, 2))
     if split:
         product_if(early, h * nx, nx // 2, 0, tokens)
     x_far_first(3)
-    y_second_if(1, 2)
+    y_second_if(5, 6)
     if split:
         product_if(early, h * nx + nx // 2, nx // 2, 0, tokens)
-    y_second_if(3, 4, 5, 6)
+    for e in events:
+        pair_in(e, (3, 4))
+    if split:
+        product_if(late, h * nx, nx, 0, tokens)
     if nh > 1:
         for k in range(far_parts):
             x_second(1 + k)
-    for e in events:
-        pair_in(e, (3, 4))
 
     body_rows = tokens - HALO
     if split:
-        product_if(late, 0, nch, body_rows, HALO)
+        product_if(None, (1 - h) * nx, nx, body_rows, HALO)
     else:
         block_product(0, body_rows, HALO)
     for tile in range(wide_all // 256):
@@ -745,7 +745,7 @@
             )
 
     if split:
-        product_if(late, 0, nch, 0, body_rows)
+        product_if(None, (1 - h) * nx, nx, 0, body_rows)
     else:
         block_product(0, 0, body_rows)
     for tile in range(wide_all // 256):
@@ -794,10 +794,8 @@
             )
             made = jnp.dot(data, toep[g], preferred_element_type=F32)
             upper = made.astype(BF16)
-            lower = (made - upper.astype(F32)).astype(BF16)
             for k, n in enumerate(blocks):
                 conv_hi[lines, n * 128 : (n + 1) * 128] = upper[k * members : (k + 1) * members]
-                conv_lo[lines, n * 128 : (n + 1) * 128] = lower[k * members : (k + 1) * members]
             return carry
 
         lax.fori_loop(0, 32, one_group, 0, unroll=4)
@@ -806,9 +804,6 @@
             cols = pl.ds(tile * 256, 256)
             made = lax.dot_general(
                 conv_hi[:, top:end], perm[:, cols], flip, preferred_element_type=F32
-            )
-            made = made + lax.dot_general(
-                conv_lo[:, top:end], perm[:, cols], flip, preferred_element_type=F32
             )
             made = made + mskip_ref[:, cols] * prod2[128 + top : 128 + end, cols].astype(F32)
             out_ref[top:end, cols] = (
@@ -862,7 +857,6 @@
     nch, nctx = nh * nx, 2 * ny * nz
     tokens, width = token_ids.shape[0], embedding.shape[1]
     piece = medium_weight.shape[0]
-    events = 1 + 2 * (nz - 1)
     hops = max(nz - 1, 1)
     vmem = pl.BlockSpec(memory_space=pltpu.VMEM)
     hbm = pl.BlockSpec(memory_space=pl.ANY)
@@ -905,12 +899,11 @@
             pltpu.VMEM((128 + tokens, width), BF16),
             pltpu.VMEM((width, 128 + tokens), BF16),
             pltpu.VMEM((width, tokens), BF16),
-            pltpu.VMEM((width, tokens), BF16),
             dma((5,)),
             dma((2,)),
             dma((2, hops, 2)),
-            dma((2, events, 4)),
-            dma((2, events, 5)),
+            dma((2, nz, 4)),
+            dma((2, nz, 5)),
             dma((2,)),
             dma((2, nz)),
             dma((2, ny)),

time: 97.6 us -> 94.4 us (0.967); the launches traced: 97.4 us -> 92.9 us
  Pallas kernels: 94.2 us -> 89.8 us
    pallas_call x1, Pallas kernels: 94.2 us -> 89.8 us  [local(): pl.pallas_call(functools.partial(kernel, sizes), out_shape=jax.ShapeDtype...]
where the time goes in v4:
time: 94.4 us; the launch traced here: 92.9 us
  Pallas kernels  89.8 us (95%)
  local copies, waits for them, and re-layouts  3.13 us (3%)
    pallas_call x1, Pallas kernels, local(): pl.pallas_call(functools.partial(kernel, sizes), out_shape=jax.ShapeDtype...  89.8 us

profile of v4, /device:TPU:49, one launch (start us, length us, event | category | flops | bytes accessed | tf_op | source)
XLA Modules:
  0.0 92.9 jit_solution(15749283431309978446)
XLA Ops:
  0.0 1.3 %broadcast_in_dim.17.gain_ref = bf16[1,512]{1,0:T(2,128)(2,1)} reshape(bf16[512]{0:T(512)(128)(2,1)} %param.20) | data formatting | bytes 2048 | tf_op jit(solution)/shard_map/broadcast_in_dim | solution.py:927
  1.3 89.8 %shard_map.127 = bf16[512,512]{1,0:T(8,128)(2,1)} custom-call(s32[1,512]{1,0:T(1,128)} %bitcast.12, bf16[512,512]{1,0:T(8,128)(2,1)} %emb_ref.1, bf16[3,512,512]{2,1,0:T(8,128)(2,1)} %bitcast.8, f32[3,3,512]{2,1,0:T(4,128)} %ltaps_ref.1, f32[16,32]{1,0:T(8,128)} %bitcast.10, f32[16,32]{1,0:T(8,128)} %bitcast.11, f32[1,512]{1,0:T(1,128)} %bitcast.13, ...), custom_call_target="tpu_custom_call" | custom-call | tf_op jit(solution)/shard_map/pallas_call | solution.py:864
  91.1 1.9 %copy.15 = bf16[512,512]{1,0:T(8,128)(2,1)} copy(bf16[512,512]{1,0:T(8,128)(2,1)} %shard_map.127) | data formatting | bytes 1048576

commit v5 on v4

--- a/solution.py
+++ b/solution.py
@@ -642,8 +642,8 @@
     y_second(0)
     far_in(2)
     x_far_first(1)
+    y_first_if(5, 6)
     far_in(3)
-    y_first_if(5, 6)
 
     for o in range(1, nch):
         origin = (ch + nch - o) % nch
@@ -702,12 +702,10 @@
     y_second_if(1, 2, 3, 4)
     for e in events:
         pair_in(e, (0, 1, 2))
-    if split:
-        product_if(early, h * nx, nx // 2, 0, tokens)
     x_far_first(3)
     y_second_if(5, 6)
     if split:
-        product_if(early, h * nx + nx // 2, nx // 2, 0, tokens)
+        product_if(early, h * nx, nx, 0, tokens)
     for e in events:
         pair_in(e, (3, 4))
     if split:

time: 94.4 us -> 94.7 us (level)
  no operation moved by 1% of the time
where the time goes in v5:
time: 94.7 us; the launch traced here: 92.9 us
  Pallas kernels  89.8 us (95%)
  local copies, waits for them, and re-layouts  3.13 us (3%)
    pallas_call x1, Pallas kernels, local(): pl.pallas_call(functools.partial(kernel, sizes), out_shape=jax.ShapeDtype...  89.8 us

profile of v5, /device:TPU:49, one launch (start us, length us, event | category | flops | bytes accessed | tf_op | source)
XLA Modules:
  0.0 92.9 jit_solution(535697507150234062)
XLA Ops:
  0.0 1.3 %broadcast_in_dim.17.gain_ref = bf16[1,512]{1,0:T(2,128)(2,1)} reshape(bf16[512]{0:T(512)(128)(2,1)} %param.20) | data formatting | bytes 2048 | tf_op jit(solution)/shard_map/broadcast_in_dim | solution.py:925
  1.3 89.8 %shard_map.127 = bf16[512,512]{1,0:T(8,128)(2,1)} custom-call(s32[1,512]{1,0:T(1,128)} %bitcast.12, bf16[512,512]{1,0:T(8,128)(2,1)} %emb_ref.1, bf16[3,512,512]{2,1,0:T(8,128)(2,1)} %bitcast.8, f32[3,3,512]{2,1,0:T(4,128)} %ltaps_ref.1, f32[16,32]{1,0:T(8,128)} %bitcast.10, f32[16,32]{1,0:T(8,128)} %bitcast.11, f32[1,512]{1,0:T(1,128)} %bitcast.13, ...), custom_call_target="tpu_custom_call" | custom-call | tf_op jit(solution)/shard_map/pallas_call | solution.py:862
  91.1 1.9 %copy.15 = bf16[512,512]{1,0:T(8,128)(2,1)} copy(bf16[512,512]{1,0:T(8,128)(2,1)} %shard_map.127) | data formatting | bytes 1048576
